TPU v7x, 256 devices: a whole 4x4x8 slice. The times are simulated.
256 devices in a mesh: dp: 32 (over z, y), tensor: 8 (over x, core).
Axes of the slice: x: 4, y: 4, z: 8, core: 2. Of those that a mesh axis runs over, the one named last changes fastest.
Arguments:
- hidden: bfloat16 [4096, 26624], P('dp', 'tensor'), may hold values from -6 to 6
- out_grad: bfloat16 [4096, 8192], P(('dp', 'tensor')), may hold values from -0.375 to 0.375
- master: float32 [8192, 26624], P('dp', 'tensor'), may hold values from -0.3125 to 0.3125
- first_moment: bfloat16 [8192, 26624], P('dp', 'tensor'), may hold values from -4 to 4
- second_moment: bfloat16 [8192, 26624], P('dp', 'tensor'), may hold values from 0.049804688 to 1
- row_counts: int32 [8], replicated, may hold values from 2816 to 3840, as said below
- step_count: int32 [1], replicated, may hold values from 1 to 11
Outputs:
- adam_update: float32 [8192, 26624], P('dp', 'tensor')
- weights_tp: bfloat16 [8192, 30720], P('dp', 'tensor')
Inputs may be any that keep to these rules, and one draw needn't show every extreme that they name: Tensor index j takes row_counts[j] consecutive hidden units in order; they sum to 26624; offsets[j] differs from j * 3328 by at most 256; the largest count equals 3840.
All inputs are finite; a program needn't handle non-finite values.
Results may differ from a plain program's by a relative error of at most 0.0045.
Values may be sent and summed in bfloat16 or wider, within the bound.
No kernel may reach another device: no remote copies, remote signals or barrier semaphores. Data moves between devices by JAX's collectives and lax.ppermute only.
A program may use at most 192 MiB of HBM per device.

v0:
```python
import jax
import jax.numpy as jnp
import numpy as np
from jax import lax
from jax.sharding import Mesh, PartitionSpec as P

DRIFT = 256
CAP = 3840
CHUNKS = ((0, 896), (2432, 3328), (896, 1664), (1664, 2432))
beta_first = 0.9
beta_second = 0.95
epsilon = 1e-08
decay_rate = 0.1
learn_rate = 0.001
TENSOR = ("x", "core")


def adamw(gradient, master, first_moment, second_moment, first_fix, second_fix):
    first_new = beta_first * first_moment + (1.0 - beta_first) * gradient
    second_new = beta_second * second_moment + (1.0 - beta_second) * gradient * gradient
    update = (
        first_new / first_fix / (jnp.sqrt(second_new / second_fix) + epsilon) + decay_rate * master
    )
    master_new = master - learn_rate * update
    return (master_new, update)


def per_device(hidden, out_grad, master, first_moment, second_moment, row_counts, step_count):
    width = hidden.shape[1]
    tensor_count = lax.axis_size(TENSOR)
    z_count = lax.axis_size("z")
    local_tokens = out_grad.shape[0]
    features = out_grad.shape[1] // z_count
    regrouped = lax.all_to_all(out_grad, "z", split_axis=1, concat_axis=0, tiled=True)
    spread = lax.all_gather(regrouped, TENSOR, axis=0, tiled=True)
    cotangent = spread.reshape(tensor_count, z_count, local_tokens, features)
    cotangent = cotangent.transpose(1, 0, 2, 3).reshape(-1, features)
    steps_done = step_count[0].astype(jnp.float32)
    first_fix = 1.0 - jnp.power(beta_first, steps_done)
    second_fix = 1.0 - jnp.power(beta_second, steps_done)
    gathered = [
        lax.all_gather(hidden[:, low:high], "z", axis=0, tiled=True) for low, high in CHUNKS
    ]
    updates = {}
    weights = {}
    for (low, high), acts in zip(CHUNKS, gathered):
        partial_value = lax.dot_general(
            cotangent, acts, (((0,), (0,)), ((), ())), preferred_element_type=jnp.float32
        ).astype(jnp.bfloat16)
        gradient = lax.psum_scatter(partial_value, "y", scatter_dimension=0, tiled=True)
        master_new, update = adamw(
            gradient.astype(jnp.float32),
            master[:, low:high],
            first_moment[:, low:high].astype(jnp.float32),
            second_moment[:, low:high].astype(jnp.float32),
            first_fix,
            second_fix,
        )
        updates[low] = update
        weights[low] = master_new.astype(jnp.bfloat16)
    order = sorted(updates)
    head = weights[order[0]][:, :DRIFT]
    tail = weights[order[-1]][:, -DRIFT:]
    ends = tensor_count - 1
    left = lax.ppermute(tail, TENSOR, [(i, i + 1) for i in range(ends)])
    right = lax.ppermute(head, TENSOR, [(i + 1, i) for i in range(ends)])
    position = lax.axis_index(TENSOR)
    places = jnp.arange(tensor_count, dtype=jnp.int32)
    first_slot = jnp.sum(jnp.where(places < position, row_counts, 0))
    length = jnp.sum(jnp.where(places == position, row_counts, 0))
    rows = master.shape[0]
    widened = jnp.concatenate(
        [left] + [weights[k] for k in order] + [right, jnp.zeros((rows, 2 * DRIFT), jnp.bfloat16)],
        axis=1,
    )
    start = first_slot - position * width + DRIFT
    window = lax.dynamic_slice_in_dim(widened, start, CAP, 1)
    slot_index = jnp.arange(CAP, dtype=jnp.int32)
    laid = jnp.where((slot_index < length)[None, :], window, jnp.zeros((), jnp.bfloat16))
    return (jnp.concatenate([updates[k] for k in order], axis=1), laid)


def solution(mesh):
    fine = Mesh(np.asarray(mesh.devices).reshape(8, 4, 4, 2), ("z", "y", "x", "core"))
    dp = ("z", "y")
    return jax.shard_map(
        per_device,
        mesh=fine,
        in_specs=(
            P(dp, TENSOR),
            P(dp + TENSOR, None),
            P(dp, TENSOR),
            P(dp, TENSOR),
            P(dp, TENSOR),
            P(),
            P(),
        ),
        out_specs=(P(dp, TENSOR), P(dp, TENSOR)),
        check_vma=False,
    )
```

profile of v0, /device:TPU:2, one launch (start us, length us, event | category | flops | bytes accessed | tf_op | source)
XLA Modules:
  0.0 358.5 jit_solution(4531047940108893145)
XLA Ops:
  7.2 0.0 all-gather.6.cloned.1.call-start
  7.2 1.0 copy.16
  8.2 20.2 %all_to_all.19 = bf16[16,8,1024]{2,0,1:T(8,128)(2,1)} all-to-all(bf16[16,8,1024]{2,0,1:T(8,128)(2,1)S(1)} %bitcast.27), channel_id=1, replica_groups=mesh['z'=8,'y'=4,'x'=4,'core'=2] {'z'}, dimensions={1} | all-to-all | bytes 524288 | tf_op jit(solution)/shard_map/all_to_all | solution.py:34
  28.4 0.0 all-gather.6.cloned.1.call-update
  28.5 0.0 all-gather.14.cloned.1.call-start
  28.5 1.9 fusion.41
  30.4 0.0 all-gather.14.cloned.1.call-update
  30.4 0.0 all-gather.8.cloned.1.call-start
  30.4 0.7 all-gather.8.cloned.1.call-update
  31.1 0.0 all-gather.10.cloned.1.call-start
  31.2 1.8 fusion.40
  33.0 0.0 all-gather.10.cloned.1.call-update
  33.0 0.0 all-gather.12.cloned.1.call-start
  33.0 0.5 all-gather.12.cloned.1.call-update
  33.6 0.0 reduce-scatter.11.cloned.1.call-start
  33.6 18.1 %all-gather.6.cloned.1.call-done = bf16[1024,1024]{1,0:T(8,128)(2,1)} async-done(((bf16[128,1024]{1,0:T(8,128)(2,1)}), bf16[1024,1024]{1,0:T(8,128)(2,1)}) %all-gather.6.cloned.1.call-update) | async-done | bytes 2097168 | tf_op jit(solution)/shard_map/all_gather | solution.py:35
  51.7 1.8 copy.13
  53.5 42.4 %all-gather.14.cloned.1.call-done = bf16[1024,896]{1,0:T(8,128)(2,1)} async-done(((bf16[128,896]{1,0:T(8,128)(2,1)}), bf16[1024,896]{1,0:T(8,128)(2,1)}) %all-gather.14.cloned.1.call-update) | async-done | bytes 1835024 | tf_op jit(solution)/shard_map/all_gather | solution.py:42
  95.9 5.1 %convolution_convert_fusion = bf16[1024,896]{1,0:T(8,128)(2,1)} fusion(bf16[1024,1024]{1,0:T(8,128)(2,1)S(1)} %bitcast.22, bf16[1024,896]{1,0:T(8,128)(2,1)} %all-gather.14.cloned.1.call-done), kind=kOutput, calls=%fused_computation.2 | convolution fusion | flops 1879965696 | bytes 5767168 | tf_op jit(solution)/shard_map/dot_general | solution.py:47
  101.0 0.0 reduce-scatter.11.cloned.1.call-update
  101.1 0.0 reduce-scatter.5.cloned.1.call-start
  101.1 36.4 %all-gather.8.cloned.1.call-done = bf16[1024,896]{1,0:T(8,128)(2,1)} async-done(((bf16[128,896]{1,0:T(8,128)(2,1)}), bf16[1024,896]{1,0:T(8,128)(2,1)}) %all-gather.8.cloned.1.call-update) | async-done | bytes 1835024 | tf_op jit(solution)/shard_map/all_gather | solution.py:42
  137.5 5.1 %convolution_convert_fusion.1 = bf16[1024,896]{1,0:T(8,128)(2,1)} fusion(bf16[1024,1024]{1,0:T(8,128)(2,1)S(1)} %bitcast.23, bf16[1024,896]{1,0:T(8,128)(2,1)} %all-gather.8.cloned.1.call-done), kind=kOutput, calls=%fused_computation.3 | convolution fusion | flops 1879965696 | bytes 5767168 | tf_op jit(solution)/shard_map/dot_general | solution.py:47
  142.6 0.0 reduce-scatter.5.cloned.1.call-update
  142.6 0.0 reduce-scatter.7.cloned.1.call-start
  142.7 35.1 %all-gather.10.cloned.1.call-done = bf16[1024,768]{1,0:T(8,128)(2,1)} async-done(((bf16[128,768]{1,0:T(8,128)(2,1)}), bf16[1024,768]{1,0:T(8,128)(2,1)}) %all-gather.10.cloned.1.call-update) | async-done | bytes 1572880 | tf_op jit(solution)/shard_map/all_gather | solution.py:42
  177.7 4.4 %convolution_convert_fusion.3 = bf16[1024,768]{1,0:T(8,128)(2,1)} fusion(bf16[1024,1024]{1,0:T(8,128)(2,1)S(1)} %bitcast.24, bf16[1024,768]{1,0:T(8,128)(2,1)} %all-gather.10.cloned.1.call-done), kind=kOutput, calls=%fused_computation.5 | convolution fusion | flops 1611399168 | bytes 5242880 | tf_op jit(solution)/shard_map/dot_general | solution.py:47
  182.1 0.0 reduce-scatter.7.cloned.1.call-update
  182.2 0.0 reduce-scatter.9.cloned.1.call-start
  182.2 35.8 %all-gather.12.cloned.1.call-done = bf16[1024,768]{1,0:T(8,128)(2,1)} async-done(((bf16[128,768]{1,0:T(8,128)(2,1)}), bf16[1024,768]{1,0:T(8,128)(2,1)}) %all-gather.12.cloned.1.call-update) | async-done | bytes 1572880 | tf_op jit(solution)/shard_map/all_gather | solution.py:42
  218.0 4.4 %convolution_convert_fusion.2 = bf16[1024,768]{1,0:T(8,128)(2,1)} fusion(bf16[1024,1024]{1,0:T(8,128)(2,1)S(1)} %bitcast.25, bf16[1024,768]{1,0:T(8,128)(2,1)} %all-gather.12.cloned.1.call-done), kind=kOutput, calls=%fused_computation.4 | convolution fusion | flops 1611399168 | bytes 5242880 | tf_op jit(solution)/shard_map/dot_general | solution.py:47
  222.4 0.0 reduce-scatter.9.cloned.1.call-update
  222.5 0.0 copy-start.1
  223.2 26.5 %reduce-scatter.11.cloned.1.call-done = bf16[256,896]{1,0:T(8,128)(2,1)} async-done(((bf16[1024,896]{1,0:T(8,128)(2,1)}), bf16[256,896]{1,0:T(8,128)(2,1)}) %reduce-scatter.11.cloned.1.call-update) | async-done | bytes 458768 | tf_op jit(solution)/shard_map/reduce_scatter | solution.py:50
  249.8 2.4 subtract_convert_fusion.1
  252.1 1.9 collective-permute-start
  254.1 0.0 copy-done.1
  254.1 0.6 fusion.34
  255.3 0.7 iota_compare_fusion
  256.0 2.5 collective-permute-done
  258.4 0.7 constant_dynamic-update-slice_fusion.3
  259.1 23.7 %reduce-scatter.5.cloned.1.call-done = bf16[256,896]{1,0:T(8,128)(2,1)} async-done(((bf16[1024,896]{1,0:T(8,128)(2,1)}), bf16[256,896]{1,0:T(8,128)(2,1)}) %reduce-scatter.5.cloned.1.call-update) | async-done | bytes 458768 | tf_op jit(solution)/shard_map/reduce_scatter | solution.py:50
  282.8 3.2 constant_dynamic-update-slice_fusion.2
  286.0 2.1 collective-permute-start.1
  288.2 25.2 %reduce-scatter.7.cloned.1.call-done = bf16[256,768]{1,0:T(8,128)(2,1)} async-done(((bf16[1024,768]{1,0:T(8,128)(2,1)}), bf16[256,768]{1,0:T(8,128)(2,1)}) %reduce-scatter.7.cloned.1.call-update) | async-done | bytes 393232 | tf_op jit(solution)/shard_map/reduce_scatter | solution.py:50
  313.3 3.0 fusion.32
  316.3 27.6 %reduce-scatter.9.cloned.1.call-done = bf16[256,768]{1,0:T(8,128)(2,1)} async-done(((bf16[1024,768]{1,0:T(8,128)(2,1)}), bf16[256,768]{1,0:T(8,128)(2,1)}) %reduce-scatter.9.cloned.1.call-update) | async-done | bytes 393232 | tf_op jit(solution)/shard_map/reduce_scatter | solution.py:50
  343.9 2.9 fusion.33
  346.9 0.0 copy-start
  346.9 2.0 pad_maximum_fusion
  348.8 0.7 copy-done
  349.6 0.0 collective-permute-done.1
  349.7 2.4 dynamic-slice_select_fusion
  (5 shorter events, 0.1 us)
Async XLA Ops:
  7.2 44.6 %all-gather.6.cloned.1.call-start = ((), (), s32[]{:S(2)}) async-start(), calls=%async_computation.5 | async-start | bytes 2359296 | tf_op jit(solution)/shard_map/all_gather | solution.py:35
  28.5 67.5 %all-gather.14.cloned.1.call-start = ((), (), s32[]{:S(2)}) async-start(), calls=%async_computation.12 | async-start | bytes 2064384 | tf_op jit(solution)/shard_map/all_gather | solution.py:42
  30.4 107.1 %all-gather.8.cloned.1.call-start = ((), (), s32[]{:S(2)}) async-start(), calls=%async_computation.6 | async-start | bytes 2064384 | tf_op jit(solution)/shard_map/all_gather | solution.py:42
  31.1 146.6 %all-gather.10.cloned.1.call-start = ((), (), s32[]{:S(2)}) async-start(), calls=%async_computation.8 | async-start | bytes 1769472 | tf_op jit(solution)/shard_map/all_gather | solution.py:42
  33.0 185.0 %all-gather.12.cloned.1.call-start = ((), (), s32[]{:S(2)}) async-start(), calls=%async_computation.10 | async-start | bytes 1769472 | tf_op jit(solution)/shard_map/all_gather | solution.py:42
  33.6 216.2 %reduce-scatter.11.cloned.1.call-start = ((), (), s32[]{:S(2)}) async-start(), calls=%async_computation.13 | async-start | bytes 2293760 | tf_op jit(solution)/shard_map/reduce_scatter | solution.py:50
  101.1 181.7 %reduce-scatter.5.cloned.1.call-start = ((), (), s32[]{:S(2)}) async-start(), calls=%async_computation.7 | async-start | bytes 2293760 | tf_op jit(solution)/shard_map/reduce_scatter | solution.py:50
  142.6 170.7 %reduce-scatter.7.cloned.1.call-start = ((), (), s32[]{:S(2)}) async-start(), calls=%async_computation.9 | async-start | bytes 1966080 | tf_op jit(solution)/shard_map/reduce_scatter | solution.py:50
  182.2 161.8 %reduce-scatter.9.cloned.1.call-start = ((), (), s32[]{:S(2)}) async-start(), calls=%async_computation.11 | async-start | bytes 1966080 | tf_op jit(solution)/shard_map/reduce_scatter | solution.py:50
  222.5 31.6 %copy-start.1 = (s32[8]{0:T(128)S(1)}, s32[8]{0:T(128)}, u32[]{:S(2)}) copy-start(s32[8]{0:T(128)} %param.12) | copy-start | bytes 100
  252.1 6.3 %collective-permute-start = (bf16[256,256]{1,0:T(8,128)(2,1)S(1)}, bf16[256,256]{1,0:T(8,128)(2,1)S(1)}, u32[]{:S(2)}, u32[]{:S(2)}) collective-permute-start(bf16[256,256]{1,0:T(8,128)(2,1)S(1)} %slice.72), channel_id=1, source_target_pairs={{0,1},{1,2},{2,3},{3,4},{4,5},{5,6},{6,7},{8,9},{9,10},{10,11},{11... | collective-permute-start | bytes 393224 | tf_op jit(solution)/shard_map/ppermute | solution.py:65
  286.0 63.6 %collective-permute-start.1 = (bf16[256,256]{1,0:T(8,128)(2,1)S(1)}, bf16[256,256]{1,0:T(8,128)(2,1)S(1)}, u32[]{:S(2)}, u32[]{:S(2)}) collective-permute-start(bf16[256,256]{1,0:T(8,128)(2,1)S(1)} %slice.73), channel_id=1, source_target_pairs={{1,0},{2,1},{3,2},{4,3},{5,4},{6,5},{7,6},{9,8},{10,9},{11,10},{12... | collective-permute-start | bytes 393224 | tf_op jit(solution)/shard_map/ppermute | solution.py:66
  346.9 2.7 copy-start
Sparse Core Ops, SparseCore 0:
  28.6 23.1 all-gather.5
  54.1 41.7 all-gather.13
  98.3 39.1 all-gather.7
  139.1 38.5 all-gather.9
  179.4 38.5 all-gather.11
  221.0 28.7 reduce-scatter.10
  252.9 29.8 reduce-scatter.4
  285.3 27.9 reduce-scatter.6
  315.9 27.9 reduce-scatter.8
where the time goes:
time: 359 us
  waiting for transfers between devices  275 us (77%)
  blocking collectives  20.2 us (6%)
  matrix products  19.1 us (5%)
  other arithmetic  17.1 us (5%)
  between operations  15.3 us (4%)
  local copies, waits for them, and re-layouts  7.9 us (2%)
  starting transfers between devices  4.42 us (1%)
    all_gather x4, waiting for transfers between devices, per_device(): lax.all_gather(hidden[:, low:high], 'z', axis=0, tiled=True)  150 us
    reduce_scatter x4, waiting for transfers between devices, per_device(): lax.psum_scatter(partial_value, 'y', scatter_dimension=0, tiled=True)  103 us
    all_to_all x1, blocking collectives, per_device(): lax.all_to_all(out_grad, 'z', split_axis=1, concat_axis=0, tiled=True)  20.2 us
    dot_general x4, matrix products, per_device(): lax.dot_general(cotangent, acts, (((0,), (0,)), ((), ())), preferred_elem...  19.1 us
    all_gather x1, waiting for transfers between devices, per_device(): spread = lax.all_gather(regrouped, TENSOR, axis=0, tiled=True)  18.1 us
    unnamed x3, other arithmetic  9.14 us
  transfers between devices with their start and end apart: 11, of which 10 were waited for; matrix products, arithmetic and copies ran while one was open for 11% of the time, Pallas kernels for 0%

commit v1 on v0

--- a/solution.py
+++ b/solution.py
@@ -31,7 +31,10 @@
     z_count = lax.axis_size("z")
     local_tokens = out_grad.shape[0]
     features = out_grad.shape[1] // z_count
-    regrouped = lax.all_to_all(out_grad, "z", split_axis=1, concat_axis=0, tiled=True)
+    regrouped = jnp.concatenate(
+        lax.all_to_all(jnp.stack(jnp.split(out_grad, lax.axis_size("z"), axis=1)), "z", 0, 0),
+        axis=0,
+    )
     spread = lax.all_gather(regrouped, TENSOR, axis=0, tiled=True)
     cotangent = spread.reshape(tensor_count, z_count, local_tokens, features)
     cotangent = cotangent.transpose(1, 0, 2, 3).reshape(-1, features)

time: 359 us -> 365 us (1.017)
  local copies, waits for them, and re-layouts: 7.9 us -> 13 us
    unnamed x7 -> x14, local copies, waits for them, and re-layouts: 1.46 us -> 6.78 us
where the time goes in v1:
time: 365 us; the launch traced here: 364 us
  waiting for transfers between devices  275 us (75%)
  blocking collectives  20.2 us (6%)
  matrix products  19.1 us (5%)
  other arithmetic  17.1 us (5%)
  between operations  15.3 us (4%)
  local copies, waits for them, and re-layouts  13 us (4%)
  starting transfers between devices  4.42 us (1%)
    all_gather x4, waiting for transfers between devices, per_device(): lax.all_gather(hidden[:, low:high], 'z', axis=0, tiled=True)  150 us
    reduce_scatter x4, waiting for transfers between devices, per_device(): lax.psum_scatter(partial_value, 'y', scatter_dimension=0, tiled=True)  103 us
    all_to_all x1, blocking collectives, per_device(): lax.all_to_all(jnp.stack(jnp.split(out_grad, lax.axis_size('z'), axis=1))...  20.2 us
    dot_general x4, matrix products, per_device(): lax.dot_general(cotangent, acts, (((0,), (0,)), ((), ())), preferred_elem...  19.1 us
    all_gather x1, waiting for transfers between devices, per_device(): spread = lax.all_gather(regrouped, TENSOR, axis=0, tiled=True)  18.1 us
    unnamed x3, other arithmetic  9.14 us
  transfers between devices with their start and end apart: 11, of which 10 were waited for; matrix products, arithmetic and copies ran while one was open for 11% of the time, Pallas kernels for 0%

profile of v1, /device:TPU:2, one launch (start us, length us, event | category | flops | bytes accessed | tf_op | source)
XLA Modules:
  0.0 363.6 jit_solution(16588130567693831979)
XLA Ops:
  7.2 0.0 all-gather.6.cloned.1.call-start
  7.2 0.8 constant_dynamic-update-slice_fusion.7
  8.0 0.8 constant_dynamic-update-slice_fusion.6
  8.7 0.8 constant_dynamic-update-slice_fusion.5
  9.5 0.8 constant_dynamic-update-slice_fusion.4
  10.3 0.8 constant_dynamic-update-slice_fusion.3
  11.0 0.8 constant_dynamic-update-slice_fusion.2
  11.8 0.8 constant_dynamic-update-slice_fusion.1
  12.5 0.8 constant_dynamic-update-slice_fusion
  13.3 20.2 %all_to_all.5 = bf16[8,16,1024]{2,1,0:T(8,128)(2,1)} all-to-all(bf16[8,16,1024]{2,1,0:T(8,128)(2,1)S(1)} %constant_dynamic-update-slice_fusion), channel_id=1, replica_groups=mesh['z'=8,'y'=4,'x'=4,'core'=2] {'z'}, dimensions={0} | all-to-all | bytes 524288 | tf_op jit(solution)/shard_map/all_to_all | solution.py:35
  33.5 0.0 all-gather.6.cloned.1.call-update
  33.6 0.0 all-gather.14.cloned.1.call-start
  33.6 1.9 fusion.41
  35.5 0.0 all-gather.14.cloned.1.call-update
  35.5 0.0 all-gather.8.cloned.1.call-start
  35.5 0.7 all-gather.8.cloned.1.call-update
  36.2 0.0 all-gather.10.cloned.1.call-start
  36.3 1.8 fusion.40
  38.1 0.0 all-gather.10.cloned.1.call-update
  38.1 0.0 all-gather.12.cloned.1.call-start
  38.1 0.5 all-gather.12.cloned.1.call-update
  38.7 0.0 reduce-scatter.11.cloned.1.call-start
  38.7 18.1 %all-gather.6.cloned.1.call-done = bf16[1024,1024]{1,0:T(8,128)(2,1)} async-done(((bf16[128,1024]{1,0:T(8,128)(2,1)}), bf16[1024,1024]{1,0:T(8,128)(2,1)}) %all-gather.6.cloned.1.call-update) | async-done | bytes 2097168 | tf_op jit(solution)/shard_map/all_gather | solution.py:38
  56.8 1.8 copy.9
  58.6 42.4 %all-gather.14.cloned.1.call-done = bf16[1024,896]{1,0:T(8,128)(2,1)} async-done(((bf16[128,896]{1,0:T(8,128)(2,1)}), bf16[1024,896]{1,0:T(8,128)(2,1)}) %all-gather.14.cloned.1.call-update) | async-done | bytes 1835024 | tf_op jit(solution)/shard_map/all_gather | solution.py:45
  101.0 5.1 %convolution_convert_fusion = bf16[1024,896]{1,0:T(8,128)(2,1)} fusion(bf16[1024,1024]{1,0:T(8,128)(2,1)S(1)} %bitcast.32, bf16[1024,896]{1,0:T(8,128)(2,1)} %all-gather.14.cloned.1.call-done), kind=kOutput, calls=%fused_computation.2 | convolution fusion | flops 1879965696 | bytes 5767168 | tf_op jit(solution)/shard_map/dot_general | solution.py:50
  106.1 0.0 reduce-scatter.11.cloned.1.call-update
  106.2 0.0 reduce-scatter.5.cloned.1.call-start
  106.2 36.4 %all-gather.8.cloned.1.call-done = bf16[1024,896]{1,0:T(8,128)(2,1)} async-done(((bf16[128,896]{1,0:T(8,128)(2,1)}), bf16[1024,896]{1,0:T(8,128)(2,1)}) %all-gather.8.cloned.1.call-update) | async-done | bytes 1835024 | tf_op jit(solution)/shard_map/all_gather | solution.py:45
  142.6 5.1 %convolution_convert_fusion.1 = bf16[1024,896]{1,0:T(8,128)(2,1)} fusion(bf16[1024,1024]{1,0:T(8,128)(2,1)S(1)} %bitcast.33, bf16[1024,896]{1,0:T(8,128)(2,1)} %all-gather.8.cloned.1.call-done), kind=kOutput, calls=%fused_computation.3 | convolution fusion | flops 1879965696 | bytes 5767168 | tf_op jit(solution)/shard_map/dot_general | solution.py:50
  147.7 0.0 reduce-scatter.5.cloned.1.call-update
  147.7 0.0 reduce-scatter.7.cloned.1.call-start
  147.8 35.1 %all-gather.10.cloned.1.call-done = bf16[1024,768]{1,0:T(8,128)(2,1)} async-done(((bf16[128,768]{1,0:T(8,128)(2,1)}), bf16[1024,768]{1,0:T(8,128)(2,1)}) %all-gather.10.cloned.1.call-update) | async-done | bytes 1572880 | tf_op jit(solution)/shard_map/all_gather | solution.py:45
  182.8 4.4 %convolution_convert_fusion.3 = bf16[1024,768]{1,0:T(8,128)(2,1)} fusion(bf16[1024,1024]{1,0:T(8,128)(2,1)S(1)} %bitcast.34, bf16[1024,768]{1,0:T(8,128)(2,1)} %all-gather.10.cloned.1.call-done), kind=kOutput, calls=%fused_computation.5 | convolution fusion | flops 1611399168 | bytes 5242880 | tf_op jit(solution)/shard_map/dot_general | solution.py:50
  187.2 0.0 reduce-scatter.7.cloned.1.call-update
  187.3 0.0 reduce-scatter.9.cloned.1.call-start
  187.3 35.8 %all-gather.12.cloned.1.call-done = bf16[1024,768]{1,0:T(8,128)(2,1)} async-done(((bf16[128,768]{1,0:T(8,128)(2,1)}), bf16[1024,768]{1,0:T(8,128)(2,1)}) %all-gather.12.cloned.1.call-update) | async-done | bytes 1572880 | tf_op jit(solution)/shard_map/all_gather | solution.py:45
  223.1 4.4 %convolution_convert_fusion.2 = bf16[1024,768]{1,0:T(8,128)(2,1)} fusion(bf16[1024,1024]{1,0:T(8,128)(2,1)S(1)} %bitcast.35, bf16[1024,768]{1,0:T(8,128)(2,1)} %all-gather.12.cloned.1.call-done), kind=kOutput, calls=%fused_computation.4 | convolution fusion | flops 1611399168 | bytes 5242880 | tf_op jit(solution)/shard_map/dot_general | solution.py:50
  227.5 0.0 reduce-scatter.9.cloned.1.call-update
  227.6 0.0 copy-start.1
  228.3 26.5 %reduce-scatter.11.cloned.1.call-done = bf16[256,896]{1,0:T(8,128)(2,1)} async-done(((bf16[1024,896]{1,0:T(8,128)(2,1)}), bf16[256,896]{1,0:T(8,128)(2,1)}) %reduce-scatter.11.cloned.1.call-update) | async-done | bytes 458768 | tf_op jit(solution)/shard_map/reduce_scatter | solution.py:53
  254.9 2.4 subtract_convert_fusion.1
  257.3 1.9 collective-permute-start
  259.2 0.0 copy-done.1
  259.2 0.6 fusion.34
  260.4 0.7 iota_compare_fusion
  261.1 2.5 collective-permute-done
  263.5 0.7 constant_dynamic-update-slice_fusion.11
  264.2 23.7 %reduce-scatter.5.cloned.1.call-done = bf16[256,896]{1,0:T(8,128)(2,1)} async-done(((bf16[1024,896]{1,0:T(8,128)(2,1)}), bf16[256,896]{1,0:T(8,128)(2,1)}) %reduce-scatter.5.cloned.1.call-update) | async-done | bytes 458768 | tf_op jit(solution)/shard_map/reduce_scatter | solution.py:53
  287.9 3.2 constant_dynamic-update-slice_fusion.10
  291.1 2.1 collective-permute-start.1
  293.3 25.2 %reduce-scatter.7.cloned.1.call-done = bf16[256,768]{1,0:T(8,128)(2,1)} async-done(((bf16[1024,768]{1,0:T(8,128)(2,1)}), bf16[256,768]{1,0:T(8,128)(2,1)}) %reduce-scatter.7.cloned.1.call-update) | async-done | bytes 393232 | tf_op jit(solution)/shard_map/reduce_scatter | solution.py:53
  318.4 3.0 fusion.32
  321.4 27.6 %reduce-scatter.9.cloned.1.call-done = bf16[256,768]{1,0:T(8,128)(2,1)} async-done(((bf16[1024,768]{1,0:T(8,128)(2,1)}), bf16[256,768]{1,0:T(8,128)(2,1)}) %reduce-scatter.9.cloned.1.call-update) | async-done | bytes 393232 | tf_op jit(solution)/shard_map/reduce_scatter | solution.py:53
  349.0 2.9 fusion.33
  352.0 0.0 copy-start
  352.0 2.0 pad_maximum_fusion
  353.9 0.7 copy-done
  354.7 0.0 collective-permute-done.1
  354.8 2.4 dynamic-slice_select_fusion
  (5 shorter events, 0.1 us)
Async XLA Ops:
  7.2 49.7 %all-gather.6.cloned.1.call-start = ((), (), s32[]{:S(2)}) async-start(), calls=%async_computation.5 | async-start | bytes 2359296 | tf_op jit(solution)/shard_map/all_gather | solution.py:38
  33.6 67.5 %all-gather.14.cloned.1.call-start = ((), (), s32[]{:S(2)}) async-start(), calls=%async_computation.12 | async-start | bytes 2064384 | tf_op jit(solution)/shard_map/all_gather | solution.py:45
  35.5 107.1 %all-gather.8.cloned.1.call-start = ((), (), s32[]{:S(2)}) async-start(), calls=%async_computation.6 | async-start | bytes 2064384 | tf_op jit(solution)/shard_map/all_gather | solution.py:45
  36.2 146.6 %all-gather.10.cloned.1.call-start = ((), (), s32[]{:S(2)}) async-start(), calls=%async_computation.8 | async-start | bytes 1769472 | tf_op jit(solution)/shard_map/all_gather | solution.py:45
  38.1 185.0 %all-gather.12.cloned.1.call-start = ((), (), s32[]{:S(2)}) async-start(), calls=%async_computation.10 | async-start | bytes 1769472 | tf_op jit(solution)/shard_map/all_gather | solution.py:45
  38.7 216.2 %reduce-scatter.11.cloned.1.call-start = ((), (), s32[]{:S(2)}) async-start(), calls=%async_computation.13 | async-start | bytes 2293760 | tf_op jit(solution)/shard_map/reduce_scatter | solution.py:53
  106.2 181.7 %reduce-scatter.5.cloned.1.call-start = ((), (), s32[]{:S(2)}) async-start(), calls=%async_computation.7 | async-start | bytes 2293760 | tf_op jit(solution)/shard_map/reduce_scatter | solution.py:53
  147.7 170.7 %reduce-scatter.7.cloned.1.call-start = ((), (), s32[]{:S(2)}) async-start(), calls=%async_computation.9 | async-start | bytes 1966080 | tf_op jit(solution)/shard_map/reduce_scatter | solution.py:53
  187.3 161.7 %reduce-scatter.9.cloned.1.call-start = ((), (), s32[]{:S(2)}) async-start(), calls=%async_computation.11 | async-start | bytes 1966080 | tf_op jit(solution)/shard_map/reduce_scatter | solution.py:53
  227.6 31.6 %copy-start.1 = (s32[8]{0:T(128)S(1)}, s32[8]{0:T(128)}, u32[]{:S(2)}) copy-start(s32[8]{0:T(128)} %param.12) | copy-start | bytes 100
  257.3 6.3 %collective-permute-start = (bf16[256,256]{1,0:T(8,128)(2,1)S(1)}, bf16[256,256]{1,0:T(8,128)(2,1)S(1)}, u32[]{:S(2)}, u32[]{:S(2)}) collective-permute-start(bf16[256,256]{1,0:T(8,128)(2,1)S(1)} %slice.72), channel_id=1, source_target_pairs={{0,1},{1,2},{2,3},{3,4},{4,5},{5,6},{6,7},{8,9},{9,10},{10,11},{11... | collective-permute-start | bytes 393224 | tf_op jit(solution)/shard_map/ppermute | solution.py:68
  291.1 63.6 %collective-permute-start.1 = (bf16[256,256]{1,0:T(8,128)(2,1)S(1)}, bf16[256,256]{1,0:T(8,128)(2,1)S(1)}, u32[]{:S(2)}, u32[]{:S(2)}) collective-permute-start(bf16[256,256]{1,0:T(8,128)(2,1)S(1)} %slice.73), channel_id=1, source_target_pairs={{1,0},{2,1},{3,2},{4,3},{5,4},{6,5},{7,6},{9,8},{10,9},{11,10},{12... | collective-permute-start | bytes 393224 | tf_op jit(solution)/shard_map/ppermute | solution.py:69
  352.0 2.7 copy-start
Sparse Core Ops, SparseCore 0:
  33.7 23.1 all-gather.5
  59.2 41.7 all-gather.13
  103.4 39.1 all-gather.7
  144.2 38.5 all-gather.9
  184.5 38.5 all-gather.11
  226.1 28.7 reduce-scatter.10
  258.0 29.8 reduce-scatter.4
  290.4 27.9 reduce-scatter.6
  321.0 27.9 reduce-scatter.8
